TPU v7x, 128 devices: a whole 4x4x4 slice. The times are simulated.
128 devices in a mesh: req: 64 (over y, x, z), head: 2 (over core).
Axes of the slice: x: 4, y: 4, z: 4, core: 2. Of those that a mesh axis runs over, the one named last changes fastest.
Arguments:
- hidden_in: bfloat16 [4096, 2048], P('req'), may hold values from -14 to 14
- attn_gain: float32 [2048], replicated, may hold values from 0.1 to 1.9
- w_query: bfloat16 [2048, 2048], P(None, 'head'), may hold values from -0.125 to 0.125
- w_key: bfloat16 [2048, 1024], P(None, 'head'), may hold values from -0.125 to 0.125
- w_value: bfloat16 [2048, 1024], P(None, 'head'), may hold values from -0.125 to 0.125
- query_gain: float32 [128], replicated, may hold values from 0.5 to 2
- key_gain: float32 [128], replicated, may hold values from 0.5 to 2
- w_out: bfloat16 [2048, 2048], P('head'), may hold values from -0.125 to 0.125
- cache_keys: bfloat16 [64, 2048, 1024], P('req', None, 'head'), may hold values from -3.5 to 3.5
- cache_values: bfloat16 [64, 2048, 1024], P('req', None, 'head'), may hold values from -6 to 6
- cache_lengths: int32 [64], replicated, may hold values from 1 to 2048, 65536 in all
- slot_request: int32 [64], replicated, may hold values from 0 to 63, each once
- mlp_gain: float32 [2048], P('head'), may hold values from 0.1 to 1.9
- w_gate: bfloat16 [2048, 6144], P('head', 'req'), may hold values from -0.125 to 0.125
- w_up: bfloat16 [2048, 6144], P('head', 'req'), may hold values from -0.125 to 0.125
- w_down: bfloat16 [6144, 2048], P('req', 'head'), may hold values from -0.078125 to 0.078125
- final_gain: float32 [2048], replicated, may hold values from 0.1 to 1.9
- w_vocab: bfloat16 [2048, 151936], P(None, ('req', 'head')), may hold values from -8 to 8
Outputs:
- hidden_out: bfloat16 [4096, 2048], P('req', 'head')
- log_probs: float32 [64, 151936], P(None, ('req', 'head'))
Inputs may be any that keep to these rules, and one draw needn't show every extreme that they name: `cache_lengths`: the largest length is exactly 2048. `slot_request`: each request appears once.
All inputs are finite; a program needn't handle non-finite values.
Results may differ from a plain program's by a relative error of at most 0.008.
Values may be sent and summed in bfloat16 or wider, within the bound.
A program may use at most 128 MiB of HBM per device.

v0:
```python
import jax
import jax.numpy as jnp
from jax import lax
from jax.sharding import PartitionSpec as P

D = 2048
HEAD_DIM = 128
EPS = 1e-06
ROPE_BASE = 1000000.0
NEG = -1e30


def norm_rows(field, gain_vec):
    return field * lax.rsqrt(jnp.mean(field * field, axis=-1, keepdims=True) + EPS) * gain_vec


def rotate(field, positions):
    half_dim = field.shape[-1] // 2
    frequency = ROPE_BASE ** (-2.0 * jnp.arange(half_dim, dtype=jnp.float32) / field.shape[-1])
    angles = positions[..., None, None] * frequency
    cosine = jnp.cos(angles)
    sines = jnp.sin(angles)
    lower_half = field[..., :half_dim]
    upper_half = field[..., half_dim:]
    return jnp.concatenate(
        [lower_half * cosine - upper_half * sines, upper_half * cosine + lower_half * sines],
        axis=-1,
    )


def inverse_order(slot_request):
    indices = jnp.arange(slot_request.shape[0], dtype=jnp.int32)
    return jnp.sum(
        jnp.where(slot_request[None, :] == indices[:, None], indices[None, :], 0), axis=1
    )


def attend_slot(queries, keys_new, values_new, keys_cache, values_cache, cache_len):
    row_count, value_heads, head_size = keys_new.shape
    group_size = queries.shape[1] // value_heads
    grouped = queries.reshape(row_count, value_heads, group_size, head_size)
    score_scale = head_size ** (-0.5)
    recent = (
        jnp.einsum("skgd,tkd->kgst", grouped, keys_new, preferred_element_type=jnp.float32)
        * score_scale
    )
    causal = jnp.arange(row_count)[:, None] >= jnp.arange(row_count)[None, :]
    recent = jnp.where(causal, recent, NEG)
    cache_span = keys_cache.shape[0]
    stored = (
        jnp.einsum("skgd,lkd->kgsl", grouped, keys_cache, preferred_element_type=jnp.float32)
        * score_scale
    )
    stored = jnp.where(jnp.arange(cache_span, dtype=jnp.int32) < cache_len, stored, NEG)
    old_weights = jnp.exp(stored)
    new_weights = jnp.exp(recent)
    row_total = jnp.sum(old_weights, axis=-1) + jnp.sum(new_weights, axis=-1)
    old_weights = (old_weights / row_total[..., None]).astype(jnp.bfloat16)
    new_weights = (new_weights / row_total[..., None]).astype(jnp.bfloat16)
    blended = jnp.einsum(
        "kgsl,lkd->skgd", old_weights, values_cache, preferred_element_type=jnp.float32
    )
    blended = blended + jnp.einsum(
        "kgst,tkd->skgd", new_weights, values_new, preferred_element_type=jnp.float32
    )
    return blended.reshape(row_count, value_heads * group_size * head_size).astype(jnp.bfloat16)


def on_device(
    hidden_in,
    attn_gain,
    w_query,
    w_key,
    w_value,
    query_gain,
    key_gain,
    w_out,
    cache_keys,
    cache_values,
    cache_lengths,
    slot_request,
    mlp_gain,
    w_gate,
    w_up,
    w_down,
    final_gain,
    w_vocab,
):
    row_count = hidden_in.shape[0]
    half_width = mlp_gain.shape[0]
    slot_index = lax.axis_index("req")
    request_id = lax.dynamic_index_in_dim(slot_request, slot_index, 0, keepdims=False)
    cache_len = lax.dynamic_index_in_dim(cache_lengths, request_id, 0, keepdims=False)
    tokens = hidden_in.astype(jnp.float32)
    normed = norm_rows(tokens, attn_gain).astype(jnp.bfloat16)
    query_heads = w_query.shape[1] // HEAD_DIM
    value_heads = w_key.shape[1] // HEAD_DIM
    positions = (cache_len + jnp.arange(row_count, dtype=jnp.int32)).astype(jnp.float32)
    queries = jnp.dot(normed, w_query, preferred_element_type=jnp.float32).reshape(
        row_count, query_heads, HEAD_DIM
    )
    queries = rotate(norm_rows(queries, query_gain), positions).astype(jnp.bfloat16)
    keys_new = jnp.dot(normed, w_key, preferred_element_type=jnp.float32).reshape(
        row_count, value_heads, HEAD_DIM
    )
    keys_new = rotate(norm_rows(keys_new, key_gain), positions).astype(jnp.bfloat16)
    values_new = (
        jnp.dot(normed, w_value, preferred_element_type=jnp.float32)
        .astype(jnp.bfloat16)
        .reshape(row_count, value_heads, HEAD_DIM)
    )
    keys_cache = cache_keys.reshape(cache_keys.shape[1], value_heads, HEAD_DIM)
    values_cache = cache_values.reshape(cache_values.shape[1], value_heads, HEAD_DIM)
    attended = attend_slot(queries, keys_new, values_new, keys_cache, values_cache, cache_len)
    projected = jnp.dot(attended, w_out, preferred_element_type=jnp.float32)
    own_sum = lax.psum_scatter(
        projected.astype(jnp.bfloat16), "head", scatter_dimension=1, tiled=True
    ).astype(jnp.float32)
    head_part = lax.axis_index("head")
    residual = lax.dynamic_slice_in_dim(tokens, head_part * half_width, half_width, 1) + own_sum
    squares = lax.psum(jnp.sum(residual * residual, axis=1), "head")
    mixed_rows = (residual * lax.rsqrt(squares[:, None] / D + EPS) * mlp_gain).astype(jnp.bfloat16)
    paired = jnp.concatenate([w_gate, w_up], axis=1)
    partial_rows = jnp.dot(
        lax.all_gather(mixed_rows, "req", axis=0, tiled=True),
        paired,
        preferred_element_type=jnp.float32,
    )
    summed_rows = lax.psum(partial_rows.astype(jnp.bfloat16), "head").astype(jnp.float32)
    unit_count = w_gate.shape[1]
    active = (jax.nn.silu(summed_rows[:, :unit_count]) * summed_rows[:, unit_count:]).astype(
        jnp.bfloat16
    )
    down_part = lax.psum_scatter(
        jnp.dot(active, w_down, preferred_element_type=jnp.float32),
        "req",
        scatter_dimension=0,
        tiled=True,
    )
    output = residual + down_part
    hidden_out = output.astype(jnp.bfloat16)
    last_row = output[row_count - 1 :, :]
    collected = lax.all_gather(last_row, ("req", "head"), axis=1, tiled=True).reshape(-1, D)
    final_rows = norm_rows(collected, final_gain).astype(jnp.bfloat16)
    logits = jnp.dot(final_rows, w_vocab, preferred_element_type=jnp.float32)
    row_max = lax.pmax(jnp.max(logits, axis=1), ("req", "head"))
    row_total = lax.psum(jnp.sum(jnp.exp(logits - row_max[:, None]), axis=1), ("req", "head"))
    log_probs = logits - row_max[:, None] - jnp.log(row_total)[:, None]
    log_probs = jnp.take(log_probs, inverse_order(slot_request), axis=0)
    return (hidden_out, log_probs)


def solution(mesh):
    in_specs = (
        P("req", None),
        P(),
        P(None, "head"),
        P(None, "head"),
        P(None, "head"),
        P(),
        P(),
        P("head", None),
        P("req", None, "head"),
        P("req", None, "head"),
        P(),
        P(),
        P("head"),
        P("head", "req"),
        P("head", "req"),
        P("req", "head"),
        P(),
        P(None, ("req", "head")),
    )
    out_specs = (P("req", "head"), P(None, ("req", "head")))
    return jax.shard_map(
        on_device, mesh=mesh, in_specs=in_specs, out_specs=out_specs, check_vma=False
    )
```

profile of v0, /device:TPU:1, one launch (start us, length us, event | category | flops | bytes accessed | tf_op | source)
XLA Modules:
  0.0 747.4 jit_solution(8484590395757010456)
XLA Ops:
  7.2 1.4 dynamic_slice.11
  10.6 1.2 dynamic_slice.12
  11.8 0.6 add_convert_fusion.2
  12.5 0.7 iota_compare_fusion.2
  13.2 1.1 multiply_reduce_fusion.1
  14.3 3.2 convolution_bitcast_fusion
  17.5 0.1 multiply_reduce_fusion.3
  17.8 0.1 copy.64
  17.9 0.2 multiply_cosine_fusion
  18.1 0.1 multiply_multiply_fusion
  18.2 0.2 subtract_convert_fusion
  18.5 4.0 reshape.165
  22.5 0.5 fusion.40
  23.0 0.1 multiply_reduce_fusion.4
  23.3 0.1 fusion.27
  23.4 0.1 subtract_convert_fusion.1
  23.5 4.1 reshape.167
  27.6 0.5 convolution_convert_fusion.2
  28.1 3.2 bitcast_reduce_fusion
  31.4 0.3 fusion.43
  31.8 1.4 fusion.12
  33.2 0.2 fusion.17
  33.4 0.1 copy.73
  33.7 3.8 convolution_convert_fusion.1
  37.6 14.1 %reduce-scatter.3.cloned.1.call-done = bf16[64,1024]{1,0:T(8,128)(2,1)} async-done(((bf16[64,2048]{1,0:T(8,128)(2,1)}), bf16[64,1024]{1,0:T(8,128)(2,1)}) %reduce-scatter.3.cloned.1.call-update) | async-done | bytes 131088 | tf_op jit(solution)/shard_map/reduce_scatter | solution.py:116
  51.6 1.0 multiply_reduce_fusion.2
  52.7 2.5 psum.21
  55.2 1.7 multiply_convert_fusion.3
  56.9 79.7 %all-gather.2.cloned.1.call-done = bf16[4096,1024]{1,0:T(8,128)(2,1)} async-done(((bf16[64,1024]{1,0:T(8,128)(2,1)}), bf16[4096,1024]{1,0:T(8,128)(2,1)}) %all-gather.2.cloned.1.call-update) | async-done | bytes 8388624 | tf_op jit(solution)/shard_map/all_gather | solution.py:125
  136.6 7.5 %convolution_convert_fusion = bf16[4096,192]{0,1:T(8,128)(2,1)} fusion(bf16[4096,1024]{1,0:T(8,128)(2,1)} %all-gather.2.cloned.1.call-done, bf16[1024,96]{0,1:T(8,128)(2,1)S(1)} %copy-done.12, bf16[1024,96]{0,1:T(8,128)(2,1)S(1)} %copy-done.13), kind=kOutput, calls=%fused_computation.1 | convolution fusion | flops 1612185600 | bytes 10354688 | tf_op jit(solution)/shard_map/dot_general | solution.py:124
  144.2 26.1 %all-reduce.2.cloned.1.call-done = bf16[4096,192]{0,1:T(8,128)(2,1)} async-done(((bf16[4096,192]{0,1:T(8,128)(2,1)}), bf16[4096,192]{0,1:T(8,128)(2,1)}) %all-reduce.2.cloned.1.call-update) | async-done | bytes 1572880 | tf_op jit(solution)/shard_map/psum | solution.py:129
  170.3 1.8 convert_element_type.67
  172.1 8.1 %fusion.18 = f32[4096,1024]{1,0:T(8,128)} fusion(bf16[96,1024]{1,0:T(8,128)(2,1)S(1)} %copy-done.6, f32[4096,192]{0,1:T(8,128)S(1)} %convert_element_type.67), kind=kOutput, calls=%fused_computation.24 | convolution fusion | flops 807665664 | bytes 20119552 | tf_op jit(solution)/shard_map/dot_general | solution.py:135
  180.2 0.6 copy-done.14
  180.9 0.1 select_reduce_fusion
  181.0 339.7 %reduce-scatter.5.cloned.1.call-done = f32[64,1024]{1,0:T(8,128)} async-done(((f32[4096,1024]{1,0:T(8,128)}), f32[64,1024]{1,0:T(8,128)}) %reduce-scatter.5.cloned.1.call-update) | async-done | bytes 262160 | tf_op jit(solution)/shard_map/reduce_scatter | solution.py:134
  520.7 1.6 fusion.41
  522.4 81.9 %all_gather.7 = f32[1,131072]{1,0:T(1,128)S(1)} all-gather(f32[1,1024]{1,0:T(1,128)S(1)} %slice.36), channel_id=1, replica_groups=mesh['req'=64,'head'=2] {'req','head'}, dimensions={1}, use_global_device_ids=true | all-gather | bytes 528384 | tf_op jit(solution)/shard_map/all_gather | solution.py:143
  604.2 0.5 broadcast.162
  604.8 1.9 reduce.3
  606.7 0.1 multiply_reduce_fusion
  606.9 4.2 fusion.44
  611.1 63.7 %pmax.7 = f32[64]{0:T(128)S(1)} all-reduce(f32[64]{0:T(128)S(1)} %get-tuple-element.14), channel_id=1, replica_groups=mesh['req'=64,'head'=2] {'req','head'}, use_global_device_ids=true, to_apply=%region_13.14 | all-reduce | flops 64 | bytes 512 | tf_op jit(solution)/shard_map/pmax | solution.py:146
  674.8 0.2 exponential_reduce_fusion
  675.0 64.2 %psum.23 = f32[64]{0:T(128)S(1)} all-reduce(f32[64]{0:T(128)S(1)} %exponential_reduce_fusion), channel_id=1, replica_groups=mesh['req'=64,'head'=2] {'req','head'}, use_global_device_ids=true, to_apply=%region_15.16 | all-reduce | flops 64 | bytes 512 | tf_op jit(solution)/shard_map/psum | solution.py:147
  739.2 0.1 subtract_subtract_fusion
  739.3 0.7 gather_fusion
  740.0 0.8 broadcast_select_fusion
  (60 shorter events, 0.9 us)
Async XLA Ops:
  7.2 15.3 %copy-start = (bf16[2048,512]{1,0:T(8,128)(2,1)S(1)}, bf16[2048,512]{1,0:T(8,128)(2,1)}, u32[]{:S(2)}) copy-start(bf16[2048,512]{1,0:T(8,128)(2,1)} %param.21) | copy-start | bytes 6291460
  7.2 10.9 %copy-start.10 = (f32[128]{0:T(128)S(1)}, f32[128]{0:T(128)}, u32[]{:S(2)}) copy-start(f32[128]{0:T(128)} %param.23) | copy-start | bytes 1540
  7.2 44.5 %reduce-scatter.3.cloned.1.call-start = ((), (), s32[]{:S(2)}) async-start(), calls=%async_computation.2 | async-start | bytes 393216 | tf_op jit(solution)/shard_map/reduce_scatter | solution.py:116
  17.7 4.8 copy-start.2
  17.7 4.8 copy-start.7
  18.4 4.8 copy-start.11
  23.0 4.6 copy-start.3
  28.1 3.6 copy-start.4
  33.6 21.6 %copy-start.9 = (f32[1024]{0:T(1024)S(1)}, f32[1024]{0:T(1024)}, u32[]{:S(2)}) copy-start(f32[1024]{0:T(1024)} %param.30) | copy-start | bytes 12292
  33.6 103.0 %copy-start.12 = (bf16[1024,96]{0,1:T(8,128)(2,1)S(1)}, bf16[1024,96]{0,1:T(8,128)(2,1)}, u32[]{:S(2)}) copy-start(bf16[1024,96]{0,1:T(8,128)(2,1)} %param.32) | copy-start | bytes 589828
  33.7 103.0 %copy-start.13 = (bf16[1024,96]{0,1:T(8,128)(2,1)S(1)}, bf16[1024,96]{0,1:T(8,128)(2,1)}, u32[]{:S(2)}) copy-start(bf16[1024,96]{0,1:T(8,128)(2,1)} %param.31) | copy-start | bytes 589828
  37.5 99.2 %all-gather.2.cloned.1.call-start = ((), (), s32[]{:S(2)}) async-start(), calls=%async_computation.3 | async-start | bytes 8519680 | tf_op jit(solution)/shard_map/all_gather | solution.py:125
  56.9 113.5 %all-reduce.2.cloned.1.call-start = ((), (), s32[]{:S(2)}) async-start(), calls=%async_computation.4 | async-start | bytes 3145728 | tf_op jit(solution)/shard_map/psum | solution.py:129
  144.2 27.9 %copy-start.6 = (bf16[96,1024]{1,0:T(8,128)(2,1)S(1)}, bf16[96,1024]{1,0:T(8,128)(2,1)}, u32[]{:S(2)}) copy-start(bf16[96,1024]{1,0:T(8,128)(2,1)} %param.33) | copy-start | bytes 589828
  144.2 376.5 %reduce-scatter.5.cloned.1.call-start = ((), (), s32[]{:S(2)}) async-start(), calls=%async_computation.5 | async-start | bytes 17039360 | tf_op jit(solution)/shard_map/reduce_scatter | solution.py:134
  180.2 0.7 copy-start.14
  180.2 340.5 %copy-start.5 = (bf16[64,1024]{1,0:T(8,128)(2,1)S(1)}, bf16[64,1024]{1,0:T(8,128)(2,1)}, u32[]{:S(2)}) copy-start(bf16[64,1024]{1,0:T(8,128)(2,1)} %reduce-scatter.3.cloned.1.call-done) | copy-start | bytes 393220
  180.9 426.0 %copy-start.8 = (f32[2048]{0:T(1024)S(1)}, f32[2048]{0:T(1024)}, u32[]{:S(2)}) copy-start(f32[2048]{0:T(1024)} %param.34) | copy-start | bytes 24580
  606.9 133.9 %copy-start.1 = (bf16[2048,512]{1,0:T(8,128)(2,1)S(1)}, bf16[2048,512]{1,0:T(8,128)(2,1)}, u32[]{:S(2)}) copy-start(bf16[2048,512]{1,0:T(8,128)(2,1)} %param.21) | copy-start | bytes 6291460
Sparse Core Ops, SparseCore 0:
  37.6 13.9 reduce-scatter.2
  57.0 79.6 all-gather.1
  144.3 25.9 all-reduce.1
  180.4 340.3 reduce-scatter.4
where the time goes:
time: 748 us; the launch traced here: 747 us
  waiting for transfers between devices  460 us (61%)
  blocking collectives  212 us (28%)
  matrix products  33.1 us (4%)
  between operations  16.1 us (2%)
  local copies, waits for them, and re-layouts  13.3 us (2%)
  other arithmetic  12.9 us (2%)
    reduce_scatter x1, waiting for transfers between devices, on_device(): lax.psum_scatter(jnp.dot(active, w_down, preferred_element_type=jnp.float...  340 us
    all_gather x1, blocking collectives, on_device(): lax.all_gather(last_row, ('req', 'head'), axis=1, tiled=True).reshape(-1, D)  81.9 us
    all_gather x1, waiting for transfers between devices, on_device(): lax.all_gather(mixed_rows, 'req', axis=0, tiled=True)  79.7 us
    psum x1, blocking collectives, on_device(): lax.psum(jnp.sum(jnp.exp(logits - row_max[:, None]), axis=1), ('req', 'he...  64.2 us
    pmax x1, blocking collectives, on_device(): row_max = lax.pmax(jnp.max(logits, axis=1), ('req', 'head'))  63.7 us
    psum x1, waiting for transfers between devices, on_device(): lax.psum(partial_rows.astype(jnp.bfloat16), 'head').astype(jnp.float32)  26.1 us
  transfers between devices with their start and end apart: 4, of which 4 were waited for; matrix products, arithmetic and copies ran while one was open for 0% of the time, Pallas kernels for 0%

commit v1 on v0

--- a/solution.py
+++ b/solution.py
@@ -8,6 +8,13 @@
 EPS = 1e-06
 ROPE_BASE = 1000000.0
 NEG = -1e30
+
+
+def exchange_gather(shard, axis, along):
+    n_dev = lax.axis_size(axis)
+    blocks = jnp.stack([shard for _ in range(n_dev)])
+    blocks = lax.all_to_all(blocks, axis, split_axis=0, concat_axis=0)
+    return jnp.concatenate(blocks, axis=along)
 
 
 def norm_rows(field, gain_vec):
@@ -122,9 +129,7 @@
     mixed_rows = (residual * lax.rsqrt(squares[:, None] / D + EPS) * mlp_gain).astype(jnp.bfloat16)
     paired = jnp.concatenate([w_gate, w_up], axis=1)
     partial_rows = jnp.dot(
-        lax.all_gather(mixed_rows, "req", axis=0, tiled=True),
-        paired,
-        preferred_element_type=jnp.float32,
+        exchange_gather(mixed_rows, "req", 0), paired, preferred_element_type=jnp.float32
     )
     summed_rows = lax.psum(partial_rows.astype(jnp.bfloat16), "head").astype(jnp.float32)
     unit_count = w_gate.shape[1]

time: 748 us -> 772 us (1.032)
  blocking collectives: 212 us -> 317 us
  waiting for transfers between devices: 460 us -> 381 us
    all_to_all x0 -> x1, blocking collectives: none -> 106 us  [exchange_gather(): blocks = lax.all_to_all(blocks, axis, split_axis=0, concat_axis=0)]
    all_gather x1 -> x0, waiting for transfers between devices: 79.7 us -> none  [on_device(): lax.all_gather(mixed_rows, 'req', axis=0, tiled=True)]
  transfers between devices with their start and end apart: 4 -> 3, of which waited for: 4 -> 3; matrix products, arithmetic and copies ran while one was open for 0% -> 0% of each run, Pallas kernels for 0% -> 0%
where the time goes in v1:
time: 772 us; the launch traced here: 771 us
  waiting for transfers between devices  381 us (49%)
  blocking collectives  317 us (41%)
  matrix products  29.6 us (4%)
  between operations  16.1 us (2%)
  local copies, waits for them, and re-layouts  14.3 us (2%)
  other arithmetic  12.2 us (2%)
    reduce_scatter x1, waiting for transfers between devices, on_device(): lax.psum_scatter(jnp.dot(active, w_down, preferred_element_type=jnp.float...  341 us
    all_to_all x1, blocking collectives, exchange_gather(): blocks = lax.all_to_all(blocks, axis, split_axis=0, concat_axis=0)  106 us
    all_gather x1, blocking collectives, on_device(): lax.all_gather(last_row, ('req', 'head'), axis=1, tiled=True).reshape(-1, D)  80.9 us
    psum x1, blocking collectives, on_device(): lax.psum(jnp.sum(jnp.exp(logits - row_max[:, None]), axis=1), ('req', 'he...  64.2 us
    pmax x1, blocking collectives, on_device(): row_max = lax.pmax(jnp.max(logits, axis=1), ('req', 'head'))  63.6 us
    psum x1, waiting for transfers between devices, on_device(): lax.psum(partial_rows.astype(jnp.bfloat16), 'head').astype(jnp.float32)  26.6 us
  transfers between devices with their start and end apart: 3, of which 3 were waited for; matrix products, arithmetic and copies ran while one was open for 0% of the time, Pallas kernels for 0%

profile of v1, /device:TPU:1, one launch (start us, length us, event | category | flops | bytes accessed | tf_op | source)
XLA Modules:
  0.0 771.1 jit_solution(12899390756968501864)
XLA Ops:
  7.2 1.4 dynamic_slice.11
  10.6 1.2 dynamic_slice.12
  11.8 0.6 add_convert_fusion.2
  12.5 0.7 iota_compare_fusion.2
  13.2 1.1 multiply_reduce_fusion.1
  14.3 3.2 convolution_bitcast_fusion
  17.5 0.1 multiply_reduce_fusion.3
  17.9 0.2 multiply_cosine_fusion
  18.1 0.1 multiply_multiply_fusion
  18.2 0.2 subtract_convert_fusion
  18.5 4.0 reshape.170
  22.5 0.5 fusion.40
  23.0 0.1 multiply_reduce_fusion.4
  23.3 0.1 fusion.27
  23.4 0.1 subtract_convert_fusion.1
  23.5 4.1 reshape.172
  27.6 0.5 convolution_convert_fusion.2
  28.1 3.2 bitcast_reduce_fusion
  31.4 0.3 fusion.43
  31.8 1.4 fusion.12
  33.2 0.2 fusion.17
  33.4 0.1 copy.73
  33.6 3.7 convolution_convert_fusion.1
  37.5 14.1 %reduce-scatter.3.cloned.1.call-done = bf16[64,1024]{1,0:T(8,128)(2,1)} async-done(((bf16[64,2048]{1,0:T(8,128)(2,1)}), bf16[64,1024]{1,0:T(8,128)(2,1)}) %reduce-scatter.3.cloned.1.call-update) | async-done | bytes 131088 | tf_op jit(solution)/shard_map/reduce_scatter | solution.py:123
  51.6 1.0 multiply_reduce_fusion.2
  52.6 2.5 psum.21
  55.1 1.0 multiply_convert_fusion.3
  56.1 1.1 stack.2
  57.2 106.0 %all_to_all.5 = bf16[64,64,1024]{2,1,0:T(8,128)(2,1)S(1)} all-to-all(bf16[64,64,1024]{2,1,0:T(8,128)(2,1)S(1)} %stack.2), channel_id=1, replica_groups=mesh['req'=64,'head'=2] {'req'}, dimensions={0} | all-to-all | bytes 16777216 | tf_op jit(solution)/shard_map/all_to_all | solution.py:16
  163.2 4.0 convolution_convert_fusion
  167.3 0.2 reduce-scatter.5.cloned.1.call-start
  167.5 26.6 %all-reduce.2.cloned.1.call-done = bf16[4096,192]{0,1:T(8,128)(2,1)} async-done(((bf16[4096,192]{0,1:T(8,128)(2,1)}), bf16[4096,192]{0,1:T(8,128)(2,1)}) %all-reduce.2.cloned.1.call-update) | async-done | bytes 1572880 | tf_op jit(solution)/shard_map/psum | solution.py:134
  194.1 1.8 convert_element_type.67
  195.9 8.1 %fusion.18 = f32[4096,1024]{1,0:T(8,128)} fusion(bf16[96,1024]{1,0:T(8,128)(2,1)S(1)} %copy-done.6, f32[4096,192]{0,1:T(8,128)S(1)} %convert_element_type.67), kind=kOutput, calls=%fused_computation.24 | convolution fusion | flops 807665664 | bytes 20119552 | tf_op jit(solution)/shard_map/dot_general | solution.py:140
  204.0 0.6 copy-done.14
  204.6 0.1 select_reduce_fusion
  204.8 340.6 %reduce-scatter.5.cloned.1.call-done = f32[64,1024]{1,0:T(8,128)} async-done(((f32[4096,1024]{1,0:T(8,128)}), f32[64,1024]{1,0:T(8,128)}) %reduce-scatter.5.cloned.1.call-update) | async-done | bytes 262160 | tf_op jit(solution)/shard_map/reduce_scatter | solution.py:139
  545.4 1.6 fusion.41
  547.0 80.9 %all_gather.3 = f32[1,131072]{1,0:T(1,128)S(1)} all-gather(f32[1,1024]{1,0:T(1,128)S(1)} %slice.36), channel_id=1, replica_groups=mesh['req'=64,'head'=2] {'req','head'}, dimensions={1}, use_global_device_ids=true | all-gather | bytes 528384 | tf_op jit(solution)/shard_map/all_gather | solution.py:148
  628.0 0.5 broadcast.164
  628.5 1.9 reduce.3
  630.5 0.1 multiply_reduce_fusion
  630.6 4.2 fusion.44
  634.8 63.6 %pmax.7 = f32[64]{0:T(128)S(1)} all-reduce(f32[64]{0:T(128)S(1)} %get-tuple-element.14), channel_id=1, replica_groups=mesh['req'=64,'head'=2] {'req','head'}, use_global_device_ids=true, to_apply=%region_13.14 | all-reduce | flops 64 | bytes 512 | tf_op jit(solution)/shard_map/pmax | solution.py:151
  698.5 0.2 exponential_reduce_fusion
  698.7 64.2 %psum.23 = f32[64]{0:T(128)S(1)} all-reduce(f32[64]{0:T(128)S(1)} %exponential_reduce_fusion), channel_id=1, replica_groups=mesh['req'=64,'head'=2] {'req','head'}, use_global_device_ids=true, to_apply=%region_15.16 | all-reduce | flops 64 | bytes 512 | tf_op jit(solution)/shard_map/psum | solution.py:152
  763.0 0.7 gather_fusion
  763.7 0.8 broadcast_select_fusion
  (59 shorter events, 1.0 us)
Async XLA Ops:
  7.2 15.3 %copy-start = (bf16[2048,512]{1,0:T(8,128)(2,1)S(1)}, bf16[2048,512]{1,0:T(8,128)(2,1)}, u32[]{:S(2)}) copy-start(bf16[2048,512]{1,0:T(8,128)(2,1)} %param.21) | copy-start | bytes 6291460
  7.2 10.9 %copy-start.10 = (f32[128]{0:T(128)S(1)}, f32[128]{0:T(128)}, u32[]{:S(2)}) copy-start(f32[128]{0:T(128)} %param.23) | copy-start | bytes 1540
  7.2 44.4 %reduce-scatter.3.cloned.1.call-start = ((), (), s32[]{:S(2)}) async-start(), calls=%async_computation.3 | async-start | bytes 393216 | tf_op jit(solution)/shard_map/reduce_scatter | solution.py:123
  17.7 4.8 copy-start.2
  17.7 4.8 copy-start.7
  18.4 4.8 copy-start.11
  23.0 4.6 copy-start.3
  28.1 3.6 copy-start.4
  33.6 21.5 %copy-start.9 = (f32[1024]{0:T(1024)S(1)}, f32[1024]{0:T(1024)}, u32[]{:S(2)}) copy-start(f32[1024]{0:T(1024)} %param.30) | copy-start | bytes 12292
  37.4 156.7 %all-reduce.2.cloned.1.call-start = ((), (), s32[]{:S(2)}) async-start(), calls=%async_computation.4 | async-start | bytes 3145728 | tf_op jit(solution)/shard_map/psum | solution.py:134
  57.2 106.0 %copy-start.12 = (bf16[1024,96]{0,1:T(8,128)(2,1)S(1)}, bf16[1024,96]{0,1:T(8,128)(2,1)}, u32[]{:S(2)}) copy-start(bf16[1024,96]{0,1:T(8,128)(2,1)} %param.32) | copy-start | bytes 589828
  57.2 106.0 %copy-start.13 = (bf16[1024,96]{0,1:T(8,128)(2,1)S(1)}, bf16[1024,96]{0,1:T(8,128)(2,1)}, u32[]{:S(2)}) copy-start(bf16[1024,96]{0,1:T(8,128)(2,1)} %param.31) | copy-start | bytes 589828
  167.2 28.6 %copy-start.6 = (bf16[96,1024]{1,0:T(8,128)(2,1)S(1)}, bf16[96,1024]{1,0:T(8,128)(2,1)}, u32[]{:S(2)}) copy-start(bf16[96,1024]{1,0:T(8,128)(2,1)} %param.33) | copy-start | bytes 589828
  167.3 378.1 %reduce-scatter.5.cloned.1.call-start = ((), (), s32[]{:S(2)}) async-start(), calls=%async_computation.5 | async-start | bytes 17039360 | tf_op jit(solution)/shard_map/reduce_scatter | solution.py:139
  204.0 0.7 copy-start.14
  204.0 341.4 %copy-start.5 = (bf16[64,1024]{1,0:T(8,128)(2,1)S(1)}, bf16[64,1024]{1,0:T(8,128)(2,1)}, u32[]{:S(2)}) copy-start(bf16[64,1024]{1,0:T(8,128)(2,1)} %reduce-scatter.3.cloned.1.call-done) | copy-start | bytes 393220
  204.6 426.0 %copy-start.8 = (f32[2048]{0:T(1024)S(1)}, f32[2048]{0:T(1024)}, u32[]{:S(2)}) copy-start(f32[2048]{0:T(1024)} %param.34) | copy-start | bytes 24580
  630.6 133.9 %copy-start.1 = (bf16[2048,512]{1,0:T(8,128)(2,1)S(1)}, bf16[2048,512]{1,0:T(8,128)(2,1)}, u32[]{:S(2)}) copy-start(bf16[2048,512]{1,0:T(8,128)(2,1)} %param.21) | copy-start | bytes 6291460
Sparse Core Ops, SparseCore 0:
  37.5 13.9 reduce-scatter.2
  167.4 26.6 all-reduce.1
  204.1 341.2 reduce-scatter.4
